TPU v7x, 512 devices: a whole 4x4x16 slice. The times are simulated.
512 devices in a mesh: ctx: 64 (over z, y), vid: 8 (over x, core).
Axes of the slice: x: 4, y: 4, z: 16, core: 2. Of those that a mesh axis runs over, the one named last changes fastest.
Arguments:
- features: bfloat16 [8, 128, 8, 32, 256], P('vid', 'ctx'), may hold values from -6 to 6
- grad_out: bfloat16 [8, 128, 8, 32, 128], P('vid', 'ctx'), may hold values from -6 to 6
- mean_saved: float32 [8, 32], P('vid'), may hold values from -3 to 3
- rstd_saved: float32 [8, 32], P('vid'), may hold values from 0.5 to 2
- latent: float32 [8, 32, 16, 16], P('vid'), may hold values from -6 to 6
- gamma: float32 [256], replicated, may hold values from 0.5 to 1.5
- beta: float32 [256], replicated, may hold values from -3 to 3
- w_scale: float32 [16, 256], replicated, may hold values from -1.5 to 1.5
- b_scale: float32 [256], replicated, may hold values from -3 to 3
- w_shift: float32 [16, 256], replicated, may hold values from -1.5 to 1.5
- b_shift: float32 [256], replicated, may hold values from -3 to 3
- kernel: bfloat16 [6912, 128], replicated, may hold values from -0.078125 to 0.078125
Outputs:
- features_grad: bfloat16 [8, 128, 8, 32, 256], P('vid', 'ctx')
- kernel_grad: float32 [6912, 128], P('ctx', 'vid')
- mod_grads: float32 [2, 16, 256], replicated
- vector_grads: float32 [4, 256], replicated
- latent_grad: float32 [8, 64, 16, 8], P('vid', 'ctx')
All inputs are finite; a program needn't handle non-finite values.
Results may differ from a plain program's by a relative error of at most 0.0029.
Values may be sent and summed in bfloat16 or wider, within the bound.
A program may use at most 64 MiB of HBM per device.

v0:
```python
import jax
import jax.numpy as jnp
from jax import lax
from jax.sharding import PartitionSpec as P

FR_DEV = 2
H = 8
W = 32
C = 256
CO = 128
G = 32
LP = 16
highest = lax.Precision.HIGHEST


def passed_along(value, axis, steps):
    count = lax.axis_size(axis)
    leading, last = (max(0, -steps), min(count, count - steps))
    return lax.ppermute(value, axis, [(source, source + steps) for source in range(leading, last)])


def swapped(value, axis, apart):
    mask = 2**apart
    pairs = [(source, source ^ mask) for source in range(lax.axis_size(axis))]
    return lax.ppermute(value, axis, pairs)


def spread_frame(table):
    grid = table.reshape(H // 4, W // 4, C)
    wide = jnp.broadcast_to(grid[:, None, :, None, :], (H // 4, 4, W // 4, 4, C))
    return wide.reshape(1, H, W, C)


def pool_frames(field):
    frames = field.shape[0]
    return field.reshape(frames, H // 4, 4, W // 4, 4, C).sum(axis=(0, 2, 4)).reshape(LP, C)


def transpose_conv(grad_pad, tap_weights, frames):
    total = jnp.zeros((frames * H * W, C), jnp.float32)
    for frame_tap in range(3):
        for row_tap in range(3):
            for col_tap in range(3):
                source = grad_pad[
                    2 - frame_tap : 2 - frame_tap + frames,
                    2 - row_tap : 2 - row_tap + H,
                    2 - col_tap : 2 - col_tap + W,
                ].reshape(frames * H * W, CO)
                total = total + lax.dot_general(
                    source,
                    tap_weights[frame_tap, row_tap, col_tap],
                    (((1,), (1,)), ((), ())),
                    preferred_element_type=jnp.float32,
                )
    return total.reshape(frames, H, W, C)


def local(
    features,
    grad_out,
    mean_saved,
    rstd_saved,
    latent,
    gamma,
    beta,
    w_scale,
    b_scale,
    w_shift,
    b_shift,
    kernel,
):
    device = lax.axis_index("ctx")
    frames_in = features[0]
    grads_in = grad_out[0]
    mean_chan = jnp.broadcast_to(mean_saved[0][:, None], (G, C // G)).reshape(C)
    rstd_chan = jnp.broadcast_to(rstd_saved[0][:, None], (G, C // G)).reshape(C)
    normed = (frames_in.astype(jnp.float32) - mean_chan) * rstd_chan
    latent_frame = lax.dynamic_index_in_dim(latent[0], device // 2, 0, keepdims=False)
    scale_tab = jnp.einsum("zp,zc->pc", latent_frame, w_scale, precision=highest) + b_scale
    shift_tab = jnp.einsum("zp,zc->pc", latent_frame, w_shift, precision=highest) + b_shift
    scale_map = spread_frame(scale_tab)
    shift_map = spread_frame(shift_tab)
    base_map = normed * gamma + beta
    modulated = base_map * scale_map + shift_map
    squashed = jax.nn.sigmoid(modulated)
    activated = (modulated * squashed).astype(jnp.bfloat16)
    before = passed_along(activated, "ctx", 1)
    leading = jnp.broadcast_to(activated[:1], before.shape)
    before = jnp.where(device == 0, leading, before)
    padded = jnp.pad(jnp.concatenate([before, activated], 0), ((0, 0), (1, 1), (1, 1), (0, 0)))
    tap_weights = kernel.reshape(3, 3, 3, C, CO)
    grads_rows = grads_in.reshape(FR_DEV * H * W, CO)
    pieces = []
    for frame_tap in range(3):
        for row_tap in range(3):
            for col_tap in range(3):
                window = padded[
                    frame_tap : frame_tap + FR_DEV, row_tap : row_tap + H, col_tap : col_tap + W
                ].reshape(FR_DEV * H * W, C)
                pieces.append(
                    lax.dot_general(
                        window,
                        grads_rows,
                        (((0,), (0,)), ((), ())),
                        preferred_element_type=jnp.float32,
                    )
                )
    kernel_term = jnp.stack(pieces).reshape(27 * C, CO)
    beyond = passed_along(grads_in, "ctx", -1)
    grad_pad = jnp.pad(jnp.concatenate([grads_in, beyond], 0), ((2, 0), (1, 1), (1, 1), (0, 0)))
    extended = transpose_conv(grad_pad, tap_weights, FR_DEV + 2)
    act_grad = extended[2:]
    virtual = jnp.where(device == 0, extended[0] + extended[1], 0.0)
    act_grad = act_grad.at[0].add(virtual)
    pre_grad = act_grad * squashed * (1.0 + modulated * (1.0 - squashed))
    features_grad = (pre_grad * scale_map * gamma * rstd_chan).astype(jnp.bfloat16)
    scale_pool = pool_frames(pre_grad * base_map)
    shift_pool = pool_frames(pre_grad)
    mod_part = jnp.stack(
        [
            jnp.einsum("zp,pc->zc", latent_frame, scale_pool, precision=highest),
            jnp.einsum("zp,pc->zc", latent_frame, shift_pool, precision=highest),
        ]
    )
    vec_part = jnp.stack(
        [
            jnp.sum(pre_grad * scale_map * normed, axis=(0, 1, 2)),
            jnp.sum(pre_grad * scale_map, axis=(0, 1, 2)),
            jnp.sum(scale_pool, axis=0),
            jnp.sum(shift_pool, axis=0),
        ]
    )
    latent_sum = jnp.einsum("zc,pc->zp", w_scale, scale_pool, precision=highest) + jnp.einsum(
        "zc,pc->zp", w_shift, shift_pool, precision=highest
    )
    half_len = LP // 2
    parity = device % 2
    own_half = lax.dynamic_slice_in_dim(latent_sum, parity * half_len, half_len, 1)
    far_half = lax.dynamic_slice_in_dim(latent_sum, (1 - parity) * half_len, half_len, 1)
    received = swapped(far_half, "ctx", 0)
    latent_grad = (own_half + received)[None, None]
    mod_grads, vector_grads = lax.psum((mod_part, vec_part), ("ctx", "vid"))
    kernel_part = lax.psum_scatter(kernel_term, "ctx", scatter_dimension=0, tiled=True)
    kernel_grad = lax.psum_scatter(kernel_part, "vid", scatter_dimension=1, tiled=True)
    return (features_grad[None], kernel_grad, mod_grads, vector_grads, latent_grad)


def solution(mesh):
    placed = (
        P("vid", "ctx", None, None, None),
        P("vid", "ctx", None, None, None),
        P("vid", None),
        P("vid", None),
        P("vid", None, None, None),
        P(),
        P(),
        P(),
        P(),
        P(),
        P(),
        P(),
    )
    return jax.shard_map(
        local,
        mesh=mesh,
        in_specs=placed,
        out_specs=(
            P("vid", "ctx", None, None, None),
            P("ctx", "vid"),
            P(),
            P(),
            P("vid", "ctx", None, None),
        ),
        check_vma=False,
    )
```

profile of v0, /device:TPU:8, one launch (start us, length us, event | category | flops | bytes accessed | tf_op | source)
XLA Modules:
  0.0 389.0 jit_solution(9092506910952850593)
XLA Ops:
  7.2 7.7 %collective-permute-start = (bf16[2,8,32,128]{3,2,1,0:T(8,128)(2,1)}, bf16[2,8,32,128]{3,2,1,0:T(8,128)(2,1)S(1)}, u32[]{:S(2)}, u32[]{:S(2)}) collective-permute-start(bf16[2,8,32,128]{3,2,1,0:T(8,128)(2,1)} %bitcast.393), channel_id=1, source_target_pairs={{8,0},{16,8},{24,16},{32,24},{40,32},{48,40},{56,48},{64,56},{72,6... | collective-permute-start | bytes 393224 | tf_op jit(solution)/shard_map/ppermute | solution.py:19
  15.2 0.9 fusion.29
  16.2 0.7 broadcast_in_dim.52
  17.0 0.7 broadcast_in_dim.54
  18.0 0.9 fusion.28
  19.0 0.9 pad_maximum_fusion.1
  20.3 0.9 pad_slice_fusion
  21.4 0.3 fusion.45
  21.7 0.3 fusion.44
  22.0 0.3 convolution_add_fusion.24
  22.3 0.3 convolution_add_fusion.23
  22.6 0.3 convolution_add_fusion.22
  22.9 0.3 fusion
  23.2 0.3 convolution_add_fusion.20
  23.5 0.3 convolution_add_fusion.19
  23.8 0.3 convolution_add_fusion.18
  24.1 0.3 convolution_add_fusion.17
  24.4 0.3 convolution_add_fusion.16
  24.7 0.3 convolution_add_fusion.15
  25.0 0.3 convolution_add_fusion.14
  25.3 0.3 convolution_add_fusion.13
  25.6 0.3 convolution_add_fusion.12
  25.9 0.3 convolution_add_fusion.11
  26.2 0.3 convolution_add_fusion.10
  26.5 0.3 convolution_add_fusion.9
  26.8 0.3 convolution_add_fusion.8
  27.1 0.3 convolution_add_fusion.7
  27.4 0.3 convolution_add_fusion.6
  27.7 0.3 convolution_add_fusion.5
  28.0 0.3 convolution_add_fusion.4
  28.3 0.3 convolution_add_fusion.3
  28.6 0.3 convolution_add_fusion.2
  28.9 0.3 convolution_add_fusion.1
  29.2 0.3 convolution_add_fusion
  29.9 0.5 fusion.42
  30.3 2.1 collective-permute-start.1
  32.5 6.1 %collective-permute-done.1 = bf16[2,8,32,256]{3,2,1,0:T(8,128)(2,1)S(1)} collective-permute-done((bf16[2,8,32,256]{3,2,1,0:T(8,128)(2,1)S(1)}, bf16[2,8,32,256]{3,2,1,0:T(8,128)(2,1)S(1)}, u32[]{:S(2)}, u32[]{:S(2)}) %collective-permute-start.1) | collective-permute-done | bytes 262176 | tf_op jit(solution)/shard_map/ppermute | solution.py:19
  39.0 0.9 pad_slice_fusion.26
  47.5 1.7 copy-done.2
  49.2 5.2 %copy.25 = f32[6912,128]{0,1:T(8,128)} copy(f32[6912,128]{1,0:T(8,128)} %bitcast.425) | data formatting | bytes 7077888 | tf_op jit(solution)/shard_map/reshape | solution.py:108
  54.5 1.3 dynamic-slice.17
  57.0 1.9 collective-permute-start.2
  59.2 109.6 %all-reduce.3 = (f32[2,16,256]{2,1,0:T(8,128)}, f32[4,256]{1,0:T(4,128)}) all-reduce(f32[2,16,256]{2,1,0:T(8,128)S(1)} %pad_maximum_fusion.2, f32[4,256]{1,0:T(4,128)S(1)} %pad_maximum_fusion.3), channel_id=1, replica_groups=mesh['ctx'=64,'vid'=8] {'ctx','vid'}, use_global_device_ids=true, to_apply=%region_6.7 | all-reduce | flops 9216 | bytes 73728 | tf_op jit(solution)/shard_map/psum | solution.py:142
  168.9 0.8 fusion.38
  169.7 174.6 %all-reduce.6.cloned.1.call-done = f32[6912,128]{0,1:T(8,128)} async-done(((f32[6912,128]{0,1:T(8,128)}), f32[6912,128]{0,1:T(8,128)}) %all-reduce.6.cloned.1.call-update) | async-done | bytes 3538960
  344.3 1.6 constant_dynamic-slice_fusion.1
  345.9 0.6 fusion.55
  346.5 35.6 %reduce-scatter.3.cloned.1.call-done = f32[108,16]{0,1:T(8,128)} async-done(((f32[108,128]{0,1:T(8,128)}), f32[108,16]{0,1:T(8,128)}) %reduce-scatter.3.cloned.1.call-update) | async-done | bytes 6928 | tf_op jit(solution)/shard_map/reduce_scatter | solution.py:144
  (78 shorter events, 10.2 us)
Async XLA Ops:
  7.2 7.8 %copy-start = (f32[1,32,16,16]{1,3,2,0:T(8,128)S(1)}, f32[1,32,16,16]{1,3,2,0:T(8,128)}, u32[]{:S(2)}) copy-start(f32[1,32,16,16]{1,3,2,0:T(8,128)} %param.18) | copy-start | bytes 98308
  7.2 337.1 %all-reduce.6.cloned.1.call-start = ((), (), s32[]{:S(2)}) async-start(), calls=%async_computation.2 | async-start | bytes 7077888
  7.2 11.8 %collective-permute-start = (bf16[2,8,32,128]{3,2,1,0:T(8,128)(2,1)}, bf16[2,8,32,128]{3,2,1,0:T(8,128)(2,1)S(1)}, u32[]{:S(2)}, u32[]{:S(2)}) collective-permute-start(bf16[2,8,32,128]{3,2,1,0:T(8,128)(2,1)} %bitcast.393), channel_id=1, source_target_pairs={{8,0},{16,8},{24,16},{32,24},{40,32},{48,40},{56,48},{64,56},{72,6... | collective-permute-start | bytes 393224 | tf_op jit(solution)/shard_map/ppermute | solution.py:19
  20.0 1.5 copy-start.3
  28.9 1.0 copy-start.4
  28.9 0.9 copy-start.7
  28.9 0.9 copy-start.8
  30.3 8.3 %collective-permute-start.1 = (bf16[2,8,32,256]{3,2,1,0:T(8,128)(2,1)S(1)}, bf16[2,8,32,256]{3,2,1,0:T(8,128)(2,1)S(1)}, u32[]{:S(2)}, u32[]{:S(2)}) collective-permute-start(bf16[2,8,32,256]{3,2,1,0:T(8,128)(2,1)S(1)} %get-tuple-element.26), channel_id=1, source_target_pairs={{0,8},{8,16},{16,24},{24,32},{32,40},{40,48},{48,56},{56,64},{64,7... | collective-permute-start | bytes 786440 | tf_op jit(solution)/shard_map/ppermute | solution.py:19
  38.7 1.2 copy-start.1
  47.4 1.8 copy-start.2
  54.4 2.3 copy-start.6
  54.4 2.5 copy-start.5
  54.4 327.8 %reduce-scatter.3.cloned.1.call-start = ((), (), s32[]{:S(2)}) async-start(), calls=%async_computation.1 | async-start | bytes 73728 | tf_op jit(solution)/shard_map/reduce_scatter | solution.py:144
  57.0 288.9 %collective-permute-start.2 = (f32[16,8]{0,1:T(8,128)S(1)}, f32[16,8]{0,1:T(8,128)S(1)}, u32[]{:S(2)}, u32[]{:S(2)}) collective-permute-start(f32[16,8]{0,1:T(8,128)S(1)} %dynamic-slice_bitcast_fusion), channel_id=1, source_target_pairs={{0,8},{8,0},{16,24},{24,16},{32,40},{40,32},{48,56},{56,48},{64,72... | collective-permute-start | bytes 1544 | tf_op jit(solution)/shard_map/ppermute | solution.py:25
Sparse Core Ops, SparseCore 0:
  54.5 289.7 all-reduce.5
  347.7 34.4 reduce-scatter.2
where the time goes:
time: 390 us; the launch traced here: 389 us
  waiting for transfers between devices  216 us (55%)
  blocking collectives  110 us (28%)
  matrix products  17.6 us (5%)
  between operations  15.5 us (4%)
  local copies, waits for them, and re-layouts  15 us (4%)
  starting transfers between devices  11.8 us (3%)
    unnamed x3, waiting for transfers between devices  175 us
    psum x1, blocking collectives, local(): mod_grads, vector_grads = lax.psum((mod_part, vec_part), ('ctx', 'vid'))  110 us
    reduce_scatter x1, waiting for transfers between devices, local(): lax.psum_scatter(kernel_part, 'vid', scatter_dimension=1, tiled=True)  35.6 us
    ppermute x2, starting transfers between devices, passed_along(): lax.ppermute(value, axis, [(source, source + steps) for source in range(l...  9.81 us
    dot_general x27, matrix products, transpose_conv(): lax.dot_general(source, tap_weights[frame_tap, row_tap, col_tap], (((1,),...  7.88 us
  transfers between devices with their start and end apart: 5, of which 3 were waited for; matrix products, arithmetic and copies ran while one was open for 2% of the time, Pallas kernels for 0%

commit v1 on v0

--- a/solution.py
+++ b/solution.py
@@ -11,6 +11,12 @@
 G = 32
 LP = 16
 highest = lax.Precision.HIGHEST
+
+
+def fix_flows(work_x):
+    for jj in ("vid", "ctx"):
+        work_x = jax.lax.psum(work_x, jj)
+    return work_x
 
 
 def passed_along(value, axis, steps):
@@ -139,7 +145,7 @@
     far_half = lax.dynamic_slice_in_dim(latent_sum, (1 - parity) * half_len, half_len, 1)
     received = swapped(far_half, "ctx", 0)
     latent_grad = (own_half + received)[None, None]
-    mod_grads, vector_grads = lax.psum((mod_part, vec_part), ("ctx", "vid"))
+    mod_grads, vector_grads = fix_flows((mod_part, vec_part))
     kernel_part = lax.psum_scatter(kernel_term, "ctx", scatter_dimension=0, tiled=True)
     kernel_grad = lax.psum_scatter(kernel_part, "vid", scatter_dimension=1, tiled=True)
     return (features_grad[None], kernel_grad, mod_grads, vector_grads, latent_grad)

time: 390 us -> 410 us (1.051)
  blocking collectives: 110 us -> 304 us
  waiting for transfers between devices: 216 us -> 42.8 us
    psum x1 -> x2, blocking collectives: 110 us -> 304 us  [fix_flows(): work_x = jax.lax.psum(work_x, jj)]
    unnamed x3, waiting for transfers between devices: 175 us -> 0.03 us
  transfers between devices with their start and end apart: 5 -> 5, of which waited for: 3 -> 2; matrix products, arithmetic and copies ran while one was open for 2% -> 2% of each run, Pallas kernels for 0% -> 0%
where the time goes in v1:
time: 410 us; the launch traced here: 409 us
  blocking collectives  304 us (74%)
  waiting for transfers between devices  42.8 us (10%)
  matrix products  17.6 us (4%)
  between operations  15.5 us (4%)
  local copies, waits for them, and re-layouts  15 us (4%)
  starting transfers between devices  11.8 us (3%)
    psum x2, blocking collectives, fix_flows(): work_x = jax.lax.psum(work_x, jj)  304 us
    reduce_scatter x1, waiting for transfers between devices, local(): lax.psum_scatter(kernel_part, 'vid', scatter_dimension=1, tiled=True)  36.6 us
    ppermute x2, starting transfers between devices, passed_along(): lax.ppermute(value, axis, [(source, source + steps) for source in range(l...  9.81 us
  transfers between devices with their start and end apart: 5, of which 2 were waited for; matrix products, arithmetic and copies ran while one was open for 2% of the time, Pallas kernels for 0%

profile of v1, /device:TPU:8, one launch (start us, length us, event | category | flops | bytes accessed | tf_op | source)
XLA Modules:
  0.0 409.4 jit_solution(18204605720327332889)
XLA Ops:
  7.2 7.7 %collective-permute-start = (bf16[2,8,32,128]{3,2,1,0:T(8,128)(2,1)}, bf16[2,8,32,128]{3,2,1,0:T(8,128)(2,1)S(1)}, u32[]{:S(2)}, u32[]{:S(2)}) collective-permute-start(bf16[2,8,32,128]{3,2,1,0:T(8,128)(2,1)} %bitcast.393), channel_id=1, source_target_pairs={{8,0},{16,8},{24,16},{32,24},{40,32},{48,40},{56,48},{64,56},{72,6... | collective-permute-start | bytes 393224 | tf_op jit(solution)/shard_map/ppermute | solution.py:25
  15.2 0.9 fusion.29
  16.2 0.7 broadcast_in_dim.52
  17.0 0.7 broadcast_in_dim.54
  18.0 0.9 fusion.28
  19.0 0.9 pad_maximum_fusion.1
  20.3 0.9 pad_slice_fusion
  21.4 0.3 fusion.45
  21.7 0.3 fusion.44
  22.0 0.3 convolution_add_fusion.24
  22.3 0.3 convolution_add_fusion.23
  22.6 0.3 convolution_add_fusion.22
  22.9 0.3 fusion
  23.2 0.3 convolution_add_fusion.20
  23.5 0.3 convolution_add_fusion.19
  23.8 0.3 convolution_add_fusion.18
  24.1 0.3 convolution_add_fusion.17
  24.4 0.3 convolution_add_fusion.16
  24.7 0.3 convolution_add_fusion.15
  25.0 0.3 convolution_add_fusion.14
  25.3 0.3 convolution_add_fusion.13
  25.6 0.3 convolution_add_fusion.12
  25.9 0.3 convolution_add_fusion.11
  26.2 0.3 convolution_add_fusion.10
  26.5 0.3 convolution_add_fusion.9
  26.8 0.3 convolution_add_fusion.8
  27.1 0.3 convolution_add_fusion.7
  27.4 0.3 convolution_add_fusion.6
  27.7 0.3 convolution_add_fusion.5
  28.0 0.3 convolution_add_fusion.4
  28.3 0.3 convolution_add_fusion.3
  28.6 0.3 convolution_add_fusion.2
  28.9 0.3 convolution_add_fusion.1
  29.2 0.3 convolution_add_fusion
  29.9 0.5 fusion.42
  30.3 2.1 collective-permute-start.1
  32.5 6.1 %collective-permute-done.1 = bf16[2,8,32,256]{3,2,1,0:T(8,128)(2,1)S(1)} collective-permute-done((bf16[2,8,32,256]{3,2,1,0:T(8,128)(2,1)S(1)}, bf16[2,8,32,256]{3,2,1,0:T(8,128)(2,1)S(1)}, u32[]{:S(2)}, u32[]{:S(2)}) %collective-permute-start.1) | collective-permute-done | bytes 262176 | tf_op jit(solution)/shard_map/ppermute | solution.py:25
  39.0 0.9 pad_slice_fusion.26
  47.5 1.7 copy-done.2
  49.2 5.2 %copy.25 = f32[6912,128]{0,1:T(8,128)} copy(f32[6912,128]{1,0:T(8,128)} %bitcast.425) | data formatting | bytes 7077888 | tf_op jit(solution)/shard_map/reshape | solution.py:114
  54.5 1.3 dynamic-slice.17
  57.0 1.9 collective-permute-start.2
  59.2 24.3 %all-reduce.4 = (f32[2,16,256]{2,1,0:T(8,128)S(1)}, f32[4,256]{1,0:T(4,128)S(1)}) all-reduce(f32[2,16,256]{2,1,0:T(8,128)S(1)} %pad_maximum_fusion.2, f32[4,256]{1,0:T(4,128)S(1)} %pad_maximum_fusion.3), channel_id=1, replica_groups=mesh['ctx'=64,'vid'=8] {'vid'}, use_global_device_ids=true, to_apply=%region_6.7 | all-reduce | flops 9216 | bytes 73728 | tf_op jit(solution)/shard_map/psum | solution.py:18
  83.6 279.4 %all-reduce.3 = (f32[2,16,256]{2,1,0:T(8,128)}, f32[4,256]{1,0:T(4,128)}) all-reduce(f32[2,16,256]{2,1,0:T(8,128)S(1)} %get-tuple-element.25, f32[4,256]{1,0:T(4,128)S(1)} %get-tuple-element.26), channel_id=1, replica_groups=mesh['ctx'=64,'vid'=8] {'ctx'}, use_global_device_ids=true, to_apply=%region_7.8 | all-reduce | flops 9216 | bytes 73728 | tf_op jit(solution)/shard_map/psum | solution.py:18
  362.9 0.8 fusion.38
  363.7 1.6 constant_dynamic-slice_fusion.1
  365.3 0.6 fusion.55
  366.0 36.6 %reduce-scatter.3.cloned.1.call-done = f32[108,16]{0,1:T(8,128)} async-done(((f32[108,128]{0,1:T(8,128)}), f32[108,16]{0,1:T(8,128)}) %reduce-scatter.3.cloned.1.call-update) | async-done | bytes 6928 | tf_op jit(solution)/shard_map/reduce_scatter | solution.py:150
  (79 shorter events, 10.2 us)
Async XLA Ops:
  7.2 7.8 %copy-start = (f32[1,32,16,16]{1,3,2,0:T(8,128)S(1)}, f32[1,32,16,16]{1,3,2,0:T(8,128)}, u32[]{:S(2)}) copy-start(f32[1,32,16,16]{1,3,2,0:T(8,128)} %param.18) | copy-start | bytes 98308
  7.2 356.5 %all-reduce.7.cloned.1.call-start = ((), (), s32[]{:S(2)}) async-start(), calls=%async_computation.2 | async-start | bytes 7077888
  7.2 11.8 %collective-permute-start = (bf16[2,8,32,128]{3,2,1,0:T(8,128)(2,1)}, bf16[2,8,32,128]{3,2,1,0:T(8,128)(2,1)S(1)}, u32[]{:S(2)}, u32[]{:S(2)}) collective-permute-start(bf16[2,8,32,128]{3,2,1,0:T(8,128)(2,1)} %bitcast.393), channel_id=1, source_target_pairs={{8,0},{16,8},{24,16},{32,24},{40,32},{48,40},{56,48},{64,56},{72,6... | collective-permute-start | bytes 393224 | tf_op jit(solution)/shard_map/ppermute | solution.py:25
  20.0 1.5 copy-start.3
  28.9 1.0 copy-start.4
  28.9 0.9 copy-start.7
  28.9 0.9 copy-start.8
  30.3 8.3 %collective-permute-start.1 = (bf16[2,8,32,256]{3,2,1,0:T(8,128)(2,1)S(1)}, bf16[2,8,32,256]{3,2,1,0:T(8,128)(2,1)S(1)}, u32[]{:S(2)}, u32[]{:S(2)}) collective-permute-start(bf16[2,8,32,256]{3,2,1,0:T(8,128)(2,1)S(1)} %get-tuple-element.28), channel_id=1, source_target_pairs={{0,8},{8,16},{16,24},{24,32},{32,40},{40,48},{48,56},{56,64},{64,7... | collective-permute-start | bytes 786440 | tf_op jit(solution)/shard_map/ppermute | solution.py:25
  38.7 1.2 copy-start.1
  47.4 1.8 copy-start.2
  54.4 2.3 copy-start.6
  54.4 2.5 copy-start.5
  54.4 348.1 %reduce-scatter.3.cloned.1.call-start = ((), (), s32[]{:S(2)}) async-start(), calls=%async_computation.1 | async-start | bytes 73728 | tf_op jit(solution)/shard_map/reduce_scatter | solution.py:150
  57.0 308.3 %collective-permute-start.2 = (f32[16,8]{0,1:T(8,128)S(1)}, f32[16,8]{0,1:T(8,128)S(1)}, u32[]{:S(2)}, u32[]{:S(2)}) collective-permute-start(f32[16,8]{0,1:T(8,128)S(1)} %dynamic-slice_bitcast_fusion), channel_id=1, source_target_pairs={{0,8},{8,0},{16,24},{24,16},{32,40},{40,32},{48,56},{56,48},{64,72... | collective-permute-start | bytes 1544 | tf_op jit(solution)/shard_map/ppermute | solution.py:31
Sparse Core Ops, SparseCore 0:
  54.5 289.5 all-reduce.6
  365.5 37.0 reduce-scatter.2
